TPU v7x, 32 devices: a whole 2x2x4 slice. The times are simulated.
32 devices in a mesh: dp: 8 (over z, x), tensor: 4 (over y, core).
Axes of the slice: x: 2, y: 2, z: 4, core: 2. Of those that a mesh axis runs over, the one named last changes fastest.
Arguments:
- context: bfloat16 [2, 8192, 3072], P(None, 'dp', 'tensor'), may hold values from -6 to 6
- out_grad: bfloat16 [2, 8192, 3072], P(None, ('dp', 'tensor')), may hold values from -0.1875 to 0.1875
- error_in: bfloat16 [2, 24576, 3072], P(None, 'dp', 'tensor'), may hold values from -6 to 6
- right_init: float32 [2, 64, 3072], P(None, None, 'tensor'), may hold values from -6 to 6
Outputs:
- summed_update: bfloat16 [2, 3072, 3072], P(None, 'dp', 'tensor')
- error_out: bfloat16 [2, 24576, 3072], P(None, 'dp', 'tensor')
All inputs are finite; a program needn't handle non-finite values.
Results may differ from a plain program's by a relative error of at most 0.015.
Values may be sent and summed in bfloat16 or wider, within the bound.
A program may use at most 128 MiB of HBM per device.

v0:
```python
import jax
import jax.numpy as jnp
from jax import lax
from jax.sharding import PartitionSpec as P


def solve_rows(gram_matrix, left_factor):
    ridge_term = 1e-06 * jnp.mean(jnp.diagonal(gram_matrix, axis1=1, axis2=2), axis=1)
    eye_matrix = jnp.eye(gram_matrix.shape[1], dtype=gram_matrix.dtype)
    gram_matrix = gram_matrix + ridge_term[:, None, None] * eye_matrix
    factor_low = jnp.linalg.cholesky(gram_matrix)

    def one_solve(low_part, rhs_part):
        return jax.scipy.linalg.solve_triangular(low_part, rhs_part, lower=True)

    return jax.vmap(one_solve)(factor_low, left_factor)


def gram_of(left_factor):
    return jnp.einsum("lrd,lsd->lrs", left_factor, left_factor, precision=lax.Precision.HIGHEST)


def compress(context, out_grad, error_in, right_init):
    out_width = out_grad.shape[2]
    moment = jnp.einsum(
        "ltd,lte->lde",
        lax.all_gather(out_grad, "tensor", axis=1, tiled=True),
        context,
        preferred_element_type=jnp.float32,
    )
    moment = moment + error_in.astype(jnp.float32)
    left_factor = jnp.einsum("lre,lde->lrd", right_init, moment, precision=lax.Precision.HIGHEST)
    left_part = lax.psum_scatter(left_factor, "tensor", scatter_dimension=2, tiled=True)
    left_part = lax.psum(left_part, "dp")
    gram_matrix = lax.psum(gram_of(left_part), "tensor")
    ortho_part = solve_rows(gram_matrix, left_part)
    ortho_basis = lax.all_gather(ortho_part, "tensor", axis=2, tiled=True)
    right_terms = jnp.einsum("lrd,lde->lre", ortho_basis, moment, precision=lax.Precision.HIGHEST)
    right_factor = lax.psum(right_terms.astype(jnp.bfloat16), "dp").astype(jnp.float32)
    replicas = lax.axis_size("dp")
    row_share = out_width // replicas
    own_basis = lax.dynamic_slice_in_dim(
        ortho_basis, lax.axis_index("dp") * row_share, row_share, 2
    )
    summed = jnp.einsum("lrd,lre->lde", own_basis, right_factor, precision=lax.Precision.HIGHEST)
    mean_part = jnp.einsum(
        "lrd,lre->lde", ortho_basis, right_factor / replicas, precision=lax.Precision.HIGHEST
    )
    new_error = (moment - mean_part).astype(jnp.bfloat16)
    return (summed.astype(jnp.bfloat16), new_error)


def body(context, out_grad, error_in, right_init):
    return compress(context, out_grad, error_in, right_init)


def solution(mesh):
    return jax.shard_map(
        body,
        mesh=mesh,
        in_specs=(
            P(None, "dp", "tensor"),
            P(None, ("dp", "tensor"), None),
            P(None, "dp", "tensor"),
            P(None, None, "tensor"),
        ),
        out_specs=(P(None, "dp", "tensor"), P(None, "dp", "tensor")),
        check_vma=False,
    )
```

profile of v0, /device:TPU:0, one launch (start us, length us, event | category | flops | bytes accessed | tf_op | source)
XLA Modules:
  0.0 419.1 jit_solution(9212171889300298580)
XLA Ops:
  7.2 0.0 copy-start
  7.2 0.0 all-gather.3.cloned.1.call-start
  7.2 4.8 %copy.12 = bf16[2,256,3072]{1,2,0:T(8,128)(2,1)} copy(bf16[2,256,3072]{2,1,0:T(8,128)(2,1)} %param.5) | data formatting | bytes 6291456 | tf_op args[1]
  12.0 0.0 all-gather.3.cloned.1.call-update
  12.0 0.0 copy-start.4
  12.0 0.0 reduce-scatter.2.cloned.1.call-start
  12.1 86.6 %all-gather.3.cloned.1.call-done = bf16[2,1024,3072]{1,2,0:T(8,128)(2,1)} async-done(((bf16[2,256,3072]{1,2,0:T(8,128)(2,1)}), bf16[2,1024,3072]{1,2,0:T(8,128)(2,1)}) %all-gather.3.cloned.1.call-update) | async-done | bytes 12582928 | tf_op jit(solution)/shard_map/all_gather | solution.py:27
  98.7 0.0 copy-done
  98.7 19.3 %convert_add_fusion = f32[2,3072,768]{2,1,0:T(8,128)} fusion(bf16[2,3072,768]{2,1,0:T(8,128)(2,1)} %param.6, bf16[2,1024,3072]{1,2,0:T(8,128)(2,1)} %all-gather.3.cloned.1.call-done, bf16[2,1024,768]{2,1,0:T(8,128)(2,1)S(1)} %copy-done), kind=kOutput, calls=%fused_computation.2 | convolution fusion | flops 9673113600 | bytes 44040192 | tf_op jit(solution)/shard_map/ltd,lte->lde/dot_general | solution.py:25
  118.0 0.0 copy-done.4
  118.0 22.5 %convolution_bitcast_fusion = f32[2,64,3072]{2,1,0:T(8,128)} fusion(f32[2,3072,768]{2,1,0:T(8,128)} %convert_add_fusion, f32[2,64,768]{2,1,0:T(8,128)S(1)} %copy-done.4), kind=kOutput, calls=%fused_computation.3 | convolution fusion | flops 3623878656 | bytes 20840448 | tf_op jit(solution)/shard_map/lre,lde->lrd/dot_general | solution.py:32
  140.5 0.0 reduce-scatter.2.cloned.1.call-update
  140.5 0.0 all-reduce.3.cloned.1.call-start
  140.5 28.1 %reduce-scatter.2.cloned.1.call-done = f32[2,64,768]{2,1,0:T(8,128)} async-done(((f32[2,64,3072]{2,1,0:T(8,128)}), f32[2,64,768]{2,1,0:T(8,128)}) %reduce-scatter.2.cloned.1.call-update) | async-done | bytes 393232 | tf_op jit(solution)/shard_map/reduce_scatter | solution.py:33
  168.6 0.0 all-reduce.3.cloned.1.call-update
  168.7 0.0 all-gather.5.cloned.1.call-start
  168.7 0.1 copy.15
  168.9 75.0 %all-reduce.3.cloned.1.call-done = f32[2,64,768]{2,1,0:T(8,128)} async-done(((f32[2,64,768]{2,1,0:T(8,128)}), f32[2,64,768]{2,1,0:T(8,128)}) %all-reduce.3.cloned.1.call-update) | async-done | bytes 393232 | tf_op jit(solution)/shard_map/psum | solution.py:34
  243.9 0.0 copy-start.2
  243.9 1.7 fusion.10
  245.5 10.9 %psum.22 = f32[2,64,64]{1,2,0:T(8,128)S(1)} all-reduce(f32[2,64,64]{1,2,0:T(8,128)S(1)} %fusion.10), channel_id=1, replica_groups=mesh['dp'=8,'tensor'=4] {'tensor'}, use_global_device_ids=true, to_apply=%region_2.0 | all-reduce | flops 8192 | bytes 65536 | tf_op jit(solution)/shard_map/psum | solution.py:35
  256.4 1.9 copy.14
  258.3 0.9 gather_fusion
  259.3 0.1 multiply_add_fusion
  259.3 0.1 copy.16
  259.4 0.1 fusion.6
  259.5 11.7 %custom-call.8 = f32[2,64,64]{2,1,0:T(8,128)S(1)} custom-call(f32[2,64,64]{2,1,0:T(8,128)S(1)} %fusion.6), custom_call_target="Cholesky" | custom-call | tf_op jit(solution)/shard_map/jit(cholesky)/cholesky | solution.py:11
  271.3 0.1 compare_reduce_fusion
  271.4 0.1 select_bitcast_fusion
  271.5 9.8 %custom-call.9 = f32[2,1,64,64]{2,3,1,0:T(8,128)S(1)} custom-call(f32[2,1,64,64]{3,2,1,0:T(8,128)S(1)} %select_bitcast_fusion), custom_call_target="InvertDiagBlocksLowerTriangular" | custom-call | tf_op jit(solution)/shard_map/vmap(jit(_solve_triangular))/triangular_solve | solution.py:14
  281.3 0.0 copy-done.2
  281.3 1.3 fusion.4
  282.6 0.0 all-gather.5.cloned.1.call-update
  282.6 0.0 all-reduce.5.cloned.1.call-start
  282.7 18.8 %all-gather.5.cloned.1.call-done = f32[2,64,3072]{2,1,0:T(8,128)} async-done(((f32[2,64,768]{2,1,0:T(8,128)}), f32[2,64,3072]{2,1,0:T(8,128)}) %all-gather.5.cloned.1.call-update) | async-done | bytes 1572880 | tf_op jit(solution)/shard_map/all_gather | solution.py:37
  301.5 16.3 %convolution_convert_fusion.1 = bf16[2,64,768]{2,1,0:T(8,128)(2,1)} fusion(f32[2,64,3072]{2,1,0:T(8,128)} %all-gather.5.cloned.1.call-done, f32[2,3072,768]{2,1,0:T(8,128)} %convert_add_fusion), kind=kOutput, calls=%fused_computation.5 | convolution fusion | flops 3623976960 | bytes 20643840 | tf_op jit(solution)/shard_map/lrd,lde->lre/dot_general | solution.py:38
  317.8 0.0 all-reduce.5.cloned.1.call-update
  317.8 70.8 %all-reduce.5.cloned.1.call-done = bf16[2,64,768]{2,1,0:T(8,128)(2,1)} async-done(((bf16[2,64,768]{2,1,0:T(8,128)(2,1)}), bf16[2,64,768]{2,1,0:T(8,128)(2,1)}) %all-reduce.5.cloned.1.call-update) | async-done | bytes 196624 | tf_op jit(solution)/shard_map/psum | solution.py:39
  388.6 0.0 copy-start.3
  388.6 0.0 copy-start.1
  388.6 20.9 %subtract_convert_fusion = bf16[2,3072,768]{2,1,0:T(8,128)(2,1)} fusion(f32[2,3072,768]{2,1,0:T(8,128)} %convert_add_fusion, f32[2,64,3072]{2,1,0:T(8,128)} %all-gather.5.cloned.1.call-done, bf16[2,64,768]{2,1,0:T(8,128)(2,1)} %all-reduce.5.cloned.1.call-done), kind=kOutput, calls=%fused_computation.1 | convolution fusion | flops 3633512448 | bytes 30081024 | tf_op jit(solution)/shard_map/lrd,lre->lde/dot_general | solution.py:46
  409.5 0.0 copy-done.3
  409.5 3.1 convolution_convert_fusion
  412.6 0.0 copy-done.1
  (7 shorter events, 0.1 us)
Async XLA Ops:
  7.2 91.5 %copy-start = (bf16[2,1024,768]{2,1,0:T(8,128)(2,1)S(1)}, bf16[2,1024,768]{2,1,0:T(8,128)(2,1)}, u32[]{:S(2)}) copy-start(bf16[2,1024,768]{2,1,0:T(8,128)(2,1)} %param.4) | copy-start | bytes 9437188
  7.2 91.5 %all-gather.3.cloned.1.call-start = ((), (), s32[]{:S(2)}) async-start(), calls=%async_computation.1 | async-start | bytes 15728640 | tf_op jit(solution)/shard_map/all_gather | solution.py:27
  12.0 105.9 %copy-start.4 = (f32[2,64,768]{2,1,0:T(8,128)S(1)}, f32[2,64,768]{2,1,0:T(8,128)}, u32[]{:S(2)}) copy-start(f32[2,64,768]{2,1,0:T(8,128)} %param.7) | copy-start | bytes 1179652
  12.0 156.6 %reduce-scatter.2.cloned.1.call-start = ((), (), s32[]{:S(2)}) async-start(), calls=%async_computation.2 | async-start | bytes 1966080 | tf_op jit(solution)/shard_map/reduce_scatter | solution.py:33
  140.5 103.4 %all-reduce.3.cloned.1.call-start = ((), (), s32[]{:S(2)}) async-start(), calls=%async_computation.3 | async-start | bytes 786432 | tf_op jit(solution)/shard_map/psum | solution.py:34
  168.7 132.8 %all-gather.5.cloned.1.call-start = ((), (), s32[]{:S(2)}) async-start(), calls=%async_computation.4 | async-start | bytes 1966080 | tf_op jit(solution)/shard_map/all_gather | solution.py:37
  243.9 37.5 %copy-start.2 = (f32[2,64,768]{2,1,0:T(8,128)S(1)}, f32[2,64,768]{2,1,0:T(8,128)}, u32[]{:S(2)}) copy-start(f32[2,64,768]{2,1,0:T(8,128)} %all-reduce.3.cloned.1.call-done) | copy-start | bytes 1179652
  282.6 106.0 %all-reduce.5.cloned.1.call-start = ((), (), s32[]{:S(2)}) async-start(), calls=%async_computation.5 | async-start | bytes 393216 | tf_op jit(solution)/shard_map/psum | solution.py:39
  388.6 20.9 %copy-start.3 = (bf16[2,64,768]{2,1,0:T(8,128)(2,1)S(1)}, bf16[2,64,768]{2,1,0:T(8,128)(2,1)}, u32[]{:S(2)}) copy-start(bf16[2,64,768]{2,1,0:T(8,128)(2,1)} %all-reduce.5.cloned.1.call-done) | copy-start | bytes 589828
  388.6 24.0 %copy-start.1 = (bf16[2,1024,768]{2,1,0:T(8,128)(2,1)S(1)}, bf16[2,1024,768]{2,1,0:T(8,128)(2,1)}, u32[]{:S(2)}) copy-start(bf16[2,1024,768]{2,1,0:T(8,128)(2,1)} %param.4) | copy-start | bytes 9437188
Sparse Core Ops, SparseCore 0:
  12.2 86.4 all-gather.2
  140.6 27.9 reduce-scatter.1
  172.0 71.8 all-reduce.2
  282.8 18.6 all-gather.4
  317.9 70.6 all-reduce.4
where the time goes:
time: 419 us
  waiting for transfers between devices  279 us (67%)
  matrix products  85 us (20%)
  other arithmetic  22 us (5%)
  between operations  13.9 us (3%)
  blocking collectives  10.9 us (3%)
  local copies, waits for them, and re-layouts  7.81 us (2%)
    all_gather x1, waiting for transfers between devices, compress(): lax.all_gather(out_grad, 'tensor', axis=1, tiled=True)  86.6 us
    psum x1, waiting for transfers between devices, compress(): left_part = lax.psum(left_part, 'dp')  75 us
    psum x1, waiting for transfers between devices, compress(): lax.psum(right_terms.astype(jnp.bfloat16), 'dp').astype(jnp.float32)  70.8 us
    reduce_scatter x1, waiting for transfers between devices, compress(): lax.psum_scatter(left_factor, 'tensor', scatter_dimension=2, tiled=True)  28.1 us
    dot_general x1, matrix products, compress(): jnp.einsum('lre,lde->lrd', right_init, moment, precision=lax.Precision.HI...  22.5 us
    dot_general x1, matrix products, compress(): jnp.einsum('lrd,lre->lde', ortho_basis, right_factor / replicas, precisio...  20.9 us
    dot_general x1, matrix products, compress(): jnp.einsum('ltd,lte->lde', lax.all_gather(out_grad, 'tensor', axis=1, til...  19.3 us
    all_gather x1, waiting for transfers between devices, compress(): ortho_basis = lax.all_gather(ortho_part, 'tensor', axis=2, tiled=True)  18.8 us
  transfers between devices with their start and end apart: 5, of which 5 were waited for; matrix products, arithmetic and copies ran while one was open for 0% of the time, Pallas kernels for 0%

commit v1 on v0

v1 whole, which is shorter than its diff:
```python
import functools

import jax
import jax.numpy as jnp
from jax import lax
from jax.experimental import pallas as pl
from jax.experimental.pallas import tpu as pltpu
from jax.sharding import PartitionSpec as P

MESH = pl.DeviceIdType.MESH
HIGHEST = lax.Precision.HIGHEST
F32 = jnp.float32
BF16 = jnp.bfloat16
LEFT_WIRE = jnp.float32
CHUNKS = 8


def split(value):
    high = value.astype(BF16)
    return high, (value - high.astype(F32)).astype(BF16)


def dot(a, b, dims):
    return lax.dot_general(a, b, (dims, ((), ())), preferred_element_type=F32)


def inverse_factors(grams):
    size = grams[0].shape[0]
    rows = lax.broadcasted_iota(jnp.int32, (size, size), 0)
    cols = lax.broadcasted_iota(jnp.int32, (size, size), 1)
    eye = (rows == cols).astype(F32)
    wide_rows = lax.broadcasted_iota(jnp.int32, (size, 2 * size), 0)
    work = []
    for gram in grams:
        mean = jnp.sum(jnp.sum(gram * eye, axis=1, keepdims=True), axis=0, keepdims=True) / size
        work.append(jnp.concatenate([gram + (1e-06 * mean) * eye, eye], axis=1))
    scales = [jnp.zeros((size, 1), F32) for _ in grams]
    one_col = wide_rows[:, :1]
    for k in range(size):
        for i, full in enumerate(work):
            row = full[k : k + 1, :]
            pivot = full[k : k + 1, k : k + 1]
            ratio = jnp.where(one_col > k, full[:, k : k + 1] / pivot, 0.0)
            scales[i] = jnp.where(one_col == k, lax.rsqrt(pivot), scales[i])
            work[i] = full - ratio * row
    return [full[:, size:] * scale for full, scale in zip(work, scales)]


def comm_kernel(
    n_d,
    n_t,
    x_hbm,
    y_hbm,
    e_hbm,
    r_hbm,
    yfull,
    ot_ref,
    right_ref,
    x_ref,
    y_ref,
    e_ref,
    r_ref,
    pt,
    pt_in,
    q_all,
    lt,
    lt_core,
    lt_send,
    lt_in,
    lt_y,
    lt_sum,
    ltf,
    r_send,
    r_in,
    r_all,
    local_sems,
    yl_sem,
    y_send,
    y_recv,
    f_send,
    f_recv,
    p_send,
    p_recv,
    c_send,
    c_recv,
    d_send,
    d_recv,
    s_send,
    s_recv,
    g_send,
    g_recv,
    h_send,
    h_recv,
    q_send,
    q_recv,
    a_send,
    a_recv,
    b_send,
    b_recv,
):
    layers, own, width = y_ref.shape
    feats = x_ref.shape[2]
    rank = r_ref.shape[1]
    d = lax.axis_index("dp")
    t = lax.axis_index("tensor")
    core = lax.rem(t, 2)
    partner = t + 1 - 2 * core
    n_y = n_t // 2
    half = width // 2
    piece = half // n_d

    def remote(src, dst, send, recv, where):
        return pltpu.make_async_remote_copy(
            src_ref=src, dst_ref=dst, send_sem=send, recv_sem=recv, device_id=where, device_id_type=MESH
        )

    loads = [
        pltpu.make_async_copy(a, b, local_sems.at[i])
        for i, (a, b) in enumerate(((r_hbm, r_ref), (x_hbm, x_ref), (y_hbm, y_ref), (e_hbm, e_ref)))
    ]
    for load in loads:
        load.start()

    barrier = pltpu.get_barrier_semaphore()
    for k in range(1, n_d):
        pl.semaphore_signal(barrier, inc=1, device_id={"dp": lax.rem(d + k, n_d)}, device_id_type=MESH)
    for k in range(1, n_t):
        pl.semaphore_signal(barrier, inc=1, device_id={"tensor": lax.rem(t + k, n_t)}, device_id_type=MESH)
    pl.semaphore_wait(barrier, n_d + n_t - 2)

    rows = own // CHUNKS
    my_rows = pl.ds(pl.multiple_of(t * own, own), own)
    chunks = [(layer, c) for layer in range(layers) for c in range(CHUNKS)]

    def chunk_copy(i, m):
        layer, c = chunks[i]
        there = lax.rem(t + 2 * m, n_t)
        return remote(
            y_hbm.at[layer, pl.ds(c * rows, rows), :],
            yfull.at[layer, pl.ds(pl.multiple_of(t * own + c * rows, rows), rows), :],
            y_send.at[m - 1, i],
            y_recv.at[m - 1, i],
            {"tensor": there},
        )

    def chunk_in(i, m):
        layer, c = chunks[i]
        source = lax.rem(t + n_t - 2 * m, n_t)
        here = yfull.at[layer, pl.ds(pl.multiple_of(source * own + c * rows, rows), rows), :]
        return here, remote(
            y_hbm.at[layer, pl.ds(c * rows, rows), :], here, y_send.at[m - 1, i], y_recv.at[m - 1, i], {"tensor": source}
        )

    def forward_copy(i, m):
        here, _ = chunk_in(i, m)
        return remote(here, here, f_send.at[m, i], f_recv.at[m, i], {"tensor": partner})

    def forward_in(i, m):
        layer, c = chunks[i]
        source = lax.rem(partner + n_t - 2 * m, n_t)
        here = yfull.at[layer, pl.ds(pl.multiple_of(source * own + c * rows, rows), rows), :]
        return remote(here, here, f_send.at[m, i], f_recv.at[m, i], {"tensor": partner})

    sent = [0]
    passed = [0]

    def send_chunks(count):
        for i in range(sent[0], min(sent[0] + count, len(chunks))):
            for m in range(1, n_y):
                chunk_copy(i, m).start()
        sent[0] = min(sent[0] + count, len(chunks))

    def pass_chunks(upto):
        for i in range(passed[0], min(upto, len(chunks))):
            for m in range(1, n_y):
                chunk_in(i, m)[1].wait_recv()
                forward_copy(i, m).start()
        passed[0] = max(passed[0], min(upto, len(chunks)))

    send_chunks(2)
    own_copy = remote(y_hbm, yfull.at[:, my_rows, :], f_send.at[0, 0], f_recv.at[0, 0], {"tensor": partner})
    own_copy.start()
    partner_rows = pl.ds(pl.multiple_of(partner * own, own), own)
    own_in = remote(y_hbm, yfull.at[:, partner_rows, :], f_send.at[0, 0], f_recv.at[0, 0], {"tensor": partner})

    loads[0].wait()
    loads[1].wait()
    r_parts = [split(r_ref[layer]) for layer in range(layers)]
    tiles = x_ref.shape[1] // own
    for tile in range(tiles):
        outs = []
        for layer in range(layers):
            block = x_ref[layer, tile * own : (tile + 1) * own, :]
            high, low = r_parts[layer]
            outs.append(dot(block, high, ((1,), (1,))) + dot(block, low, ((1,), (1,))))
        pt[tile] = jnp.concatenate(outs, axis=1)

    p_out = []
    for k in range(1, n_t):
        there = lax.rem(t + k, n_t)
        copy = remote(pt.at[there], pt_in.at[k - 1], p_send.at[k - 1], p_recv.at[k - 1], {"tensor": there})
        copy.start()
        p_out.append(copy)
    send_chunks(3)

    loads[3].wait()
    loads[2].wait()
    own_y = pltpu.make_async_copy(y_ref, yfull.at[:, my_rows, :], yl_sem)
    own_y.start()
    block_rows = width // 6

    def left_of_error(i, carry):
        at = pl.ds(pl.multiple_of(i * block_rows, block_rows), block_rows)
        outs = []
        for layer in range(layers):
            block = e_ref[layer, at, :]
            high, low = r_parts[layer]
            outs.append(dot(block, high, ((1,), (1,))) + dot(block, low, ((1,), (1,))))
        lt[at, :] = jnp.concatenate(outs, axis=1)
        return carry

    lax.fori_loop(0, 6, left_of_error, 0)
    for copy in p_out:
        copy.wait()
    total = pt[t]
    for k in range(n_t - 1):
        total = total + pt_in[k]
    p_parts = [split(total[:, layer * rank : (layer + 1) * rank]) for layer in range(layers)]

    def left_of_tokens(i, carry):
        at = pl.ds(pl.multiple_of(i * block_rows, block_rows), block_rows)
        outs = []
        for layer in range(layers):
            block = y_ref[layer, :, at]
            high, low = p_parts[layer]
            outs.append(dot(block, high, ((0,), (0,))) + dot(block, low, ((0,), (0,))))
        lt[at, :] += jnp.concatenate(outs, axis=1)
        return carry

    lax.fori_loop(0, 6, left_of_tokens, 0)

    mine = pl.multiple_of(core * half, half)
    other = pl.multiple_of((1 - core) * half, half)
    core_copy = remote(lt.at[pl.ds(other, half), :], lt_core, c_send, c_recv, {"tensor": partner})
    core_copy.start()
    core_copy.wait()

    def add_core(j, carry):
        at = pl.ds(pl.multiple_of(mine + j * piece, piece), piece)
        value = lt[at, :] + lt_core[pl.ds(pl.multiple_of(j * piece, piece), piece), :]
        lt_send[j] = value.astype(lt_send.dtype)
        return carry

    lax.fori_loop(0, n_d, add_core, 0)
    d_out = []
    for k in range(1, n_d):
        there = lax.rem(d + k, n_d)
        copy = remote(lt_send.at[there], lt_in.at[k - 1], d_send.at[k - 1], d_recv.at[k - 1], {"dp": there})
        copy.start()
        d_out.append(copy)
    send_chunks(4)
    pass_chunks(2)
    for copy in d_out:
        copy.wait()
    total = lt_send[d].astype(F32)
    for k in range(n_d - 1):
        total = total + lt_in[k].astype(F32)
    lt_sum[...] = total
    s_out = []
    for m in range(1, n_y):
        there = lax.rem(t + 2 * m, n_t)
        copy = remote(lt_sum, lt_y.at[m - 1], s_send.at[m - 1], s_recv.at[m - 1], {"tensor": there})
        copy.start()
        s_out.append(copy)
    send_chunks(3)
    for copy in s_out:
        copy.wait()
    for m in range(n_y - 1):
        total = total + lt_y[m]

    def slot(side, index):
        return ltf.at[pl.ds(pl.multiple_of(side * half + index * piece, piece), piece), :]

    ltf[pl.ds(pl.multiple_of(mine + d * piece, piece), piece), :] = total.astype(ltf.dtype)
    g_out = []
    for k in range(1, n_d):
        there = lax.rem(d + k, n_d)
        copy = remote(slot(core, d), slot(core, d), g_send.at[k - 1], g_recv.at[k - 1], {"dp": there})
        copy.start()
        g_out.append(copy)
    h_out = []
    for k in range(n_d):
        source = lax.rem(d + n_d - k, n_d)
        if k > 0:
            remote(slot(core, source), slot(core, source), g_send.at[k - 1], g_recv.at[k - 1], {"dp": source}).wait_recv()
        copy = remote(slot(core, source), slot(core, source), h_send.at[k], h_recv.at[k], {"tensor": partner})
        copy.start()
        h_out.append(copy)
    send_chunks(3)
    pass_chunks(7)
    for k in range(n_d):
        source = lax.rem(d + n_d - k, n_d)
        remote(
            slot(1 - core, source), slot(1 - core, source), h_send.at[k], h_recv.at[k], {"tensor": partner}
        ).wait_recv()
    for copy in g_out + h_out:
        copy.wait_send()

    gram = jnp.zeros((layers * rank, layers * rank), F32)
    for i in range(6):
        block = ltf[i * block_rows : (i + 1) * block_rows, :].astype(F32)
        gram = gram + lax.dot_general(
            block, block, (((0,), (0,)), ((), ())), precision=HIGHEST, preferred_element_type=F32
        )
    grams = [gram[k * rank : (k + 1) * rank, k * rank : (k + 1) * rank] for k in range(layers)]
    inverses = inverse_factors(grams)
    zero = jnp.zeros((rank, rank), F32)
    spread = jnp.concatenate(
        [
            jnp.concatenate([inverses[i] if i == j else zero for j in range(layers)], axis=1)
            for i in range(layers)
        ],
        axis=0,
    )

    q = [jnp.zeros((own, 2 * rank), F32) for _ in range(layers)]
    right = [jnp.zeros((2 * rank, feats), F32) for _ in range(layers)]
    for i in range(6):
        at = slice(i * block_rows, (i + 1) * block_rows)
        basis = lax.dot_general(
            ltf[at, :].astype(F32), spread, (((1,), (1,)), ((), ())), precision=HIGHEST, preferred_element_type=F32
        )
        ot_ref[at, :] = basis
        for layer in range(layers):
            both = jnp.concatenate(split(basis[:, layer * rank : (layer + 1) * rank]), axis=1)
            q[layer] = q[layer] + dot(y_ref[layer, :, at], both, ((1,), (0,)))
    q_all[t] = jnp.concatenate([part[:, :rank] + part[:, rank:] for part in q], axis=1)
    q_out = []
    for k in range(1, n_t):
        copy = remote(
            q_all.at[t], q_all.at[t], q_send.at[k - 1], q_recv.at[k - 1], {"tensor": lax.rem(t + k, n_t)}
        )
        copy.start()
        q_out.append(copy)
    send_chunks(len(chunks))
    for i in range(6):
        at = slice(i * block_rows, (i + 1) * block_rows)
        for layer in range(layers):
            both = jnp.concatenate(split(ot_ref[at, layer * rank : (layer + 1) * rank]), axis=1)
            right[layer] = right[layer] + dot(both, e_ref[layer, at, :], ((0,), (0,)))
    for k in range(1, n_t):
        source = lax.rem(t + n_t - k, n_t)
        remote(
            q_all.at[source], q_all.at[source], q_send.at[k - 1], q_recv.at[k - 1], {"tensor": source}
        ).wait_recv()
    for tile in range(tiles):
        value = q_all[tile]
        for layer in range(layers):
            both = jnp.concatenate(split(value[:, layer * rank : (layer + 1) * rank]), axis=1)
            right[layer] = right[layer] + dot(both, x_ref[layer, tile * own : (tile + 1) * own, :], ((0,), (0,)))
    right_rows = jnp.concatenate([part[:rank] + part[rank:] for part in right], axis=0)
    share = layers * rank // n_d
    for j in range(n_d):
        r_send[j] = right_rows[j * share : (j + 1) * share, :].astype(BF16)
    a_out = []
    for k in range(1, n_d):
        there = lax.rem(d + k, n_d)
        copy = remote(r_send.at[there], r_in.at[k - 1], a_send.at[k - 1], a_recv.at[k - 1], {"dp": there})
        copy.start()
        a_out.append(copy)
    pass_chunks(10)
    for copy in a_out:
        copy.wait()
    total = r_send[d].astype(F32)
    for k in range(n_d - 1):
        total = total + r_in[k].astype(F32)
    r_all[d] = total.astype(BF16)
    b_out = []
    for k in range(1, n_d):
        copy = remote(r_all.at[d], r_all.at[d], b_send.at[k - 1], b_recv.at[k - 1], {"dp": lax.rem(d + k, n_d)})
        copy.start()
        b_out.append(copy)
    pass_chunks(len(chunks))
    for k in range(1, n_d):
        source = lax.rem(d + n_d - k, n_d)
        remote(r_all.at[source], r_all.at[source], b_send.at[k - 1], b_recv.at[k - 1], {"dp": source}).wait_recv()
    right_ref[...] = r_all[...]
    own_in.wait_recv()
    own_copy.wait_send()
    own_y.wait()
    for copy in q_out + b_out:
        copy.wait_send()
    for i in range(len(chunks)):
        for m in range(1, n_y):
            chunk_copy(i, m).wait_send()
            forward_copy(i, m).wait_send()
            forward_in(i, m).wait_recv()


def error_kernel(n_d, y_ref, x_ref, e_ref, o_ref, r_ref, own_ref, err_ref, sum_ref):
    layer = pl.program_id(0)
    rank = r_ref.shape[1]

    def low_rank(basis):
        high, low = split(basis)
        return dot(high, r_ref[0], ((1,), (0,))) + dot(low, r_ref[0], ((1,), (0,)))

    moment = dot(y_ref[0], x_ref[0], ((0,), (0,))) + e_ref[0].astype(F32)
    err_ref[0] = (moment - low_rank(o_ref[0]) * (1.0 / n_d)).astype(err_ref.dtype)

    @pl.when(pl.program_id(1) == 0)
    def _():
        sum_ref[0] = low_rank(own_ref[0]).astype(sum_ref.dtype)


def solution(mesh):
    n_d, n_t = mesh.shape["dp"], mesh.shape["tensor"]

    def body(context, out_grad, error_in, right_init):
        layers, tokens, feats = context.shape
        own, width = out_grad.shape[1:]
        rank = right_init.shape[1]
        wide = layers * rank
        half = width // 2
        piece = half // n_d
        share = wide // n_d
        n_y = n_t // 2
        n_c = layers * CHUNKS
        dma = pltpu.SemaphoreType.DMA
        any_spec = pl.BlockSpec(memory_space=pl.ANY)
        vmem_spec = pl.BlockSpec(memory_space=pltpu.VMEM)
        pairs = lambda *shape: [dma(shape), dma(shape)]
        yfull, ortho, right = pl.pallas_call(
            functools.partial(comm_kernel, n_d, n_t),
            name="low_rank_chain",
            out_shape=(
                jax.ShapeDtypeStruct((layers, tokens, width), BF16),
                jax.ShapeDtypeStruct((width, wide), F32),
                jax.ShapeDtypeStruct((n_d, share, feats), BF16),
            ),
            in_specs=[any_spec] * 4,
            out_specs=(any_spec, vmem_spec, vmem_spec),
            scratch_shapes=[
                pltpu.VMEM((layers, tokens, feats), BF16),
                pltpu.VMEM((layers, own, width), BF16),
                pltpu.VMEM((layers, width, feats), BF16),
                pltpu.VMEM((layers, rank, feats), F32),
                pltpu.VMEM((n_t, own, wide), F32),
                pltpu.VMEM((n_t - 1, own, wide), F32),
                pltpu.VMEM((n_t, own, wide), F32),
                pltpu.VMEM((width, wide), F32),
                pltpu.VMEM((half, wide), F32),
                pltpu.VMEM((n_d, piece, wide), LEFT_WIRE),
                pltpu.VMEM((n_d - 1, piece, wide), LEFT_WIRE),
                pltpu.VMEM((max(n_y - 1, 1), piece, wide), F32),
                pltpu.VMEM((piece, wide), F32),
                pltpu.VMEM((width, wide), LEFT_WIRE),
                pltpu.VMEM((n_d, share, feats), BF16),
                pltpu.VMEM((n_d - 1, share, feats), BF16),
                pltpu.VMEM((n_d, share, feats), BF16),
                dma((4,)),
                dma,
            ]
            + pairs(max(n_y - 1, 1), n_c)
            + pairs(n_y, n_c)
            + pairs(n_t - 1)
            + [dma, dma]
            + pairs(n_d - 1)
            + pairs(max(n_y - 1, 1))
            + pairs(n_d - 1)
            + pairs(n_d)
            + pairs(n_t - 1)
            + pairs(n_d - 1)
            + pairs(n_d - 1),
            compiler_params=pltpu.CompilerParams(
                collective_id=0, has_side_effects=True, vmem_limit_bytes=60 * 1024 * 1024
            ),
        )(context, out_grad, error_in, right_init)
        ortho = jnp.transpose(ortho.reshape(width, layers, rank), (1, 0, 2))
        right = right.reshape(layers, rank, feats)
        rows = width // n_d
        own_basis = lax.dynamic_slice_in_dim(ortho, lax.axis_index("dp") * rows, rows, 1)
        tile = width // 6
        new_error, summed = pl.pallas_call(
            functools.partial(error_kernel, n_d),
            name="new_error",
            grid=(layers, width // tile),
            out_shape=(
                jax.ShapeDtypeStruct((layers, width, feats), BF16),
                jax.ShapeDtypeStruct((layers, rows, feats), BF16),
            ),
            in_specs=[
                pl.BlockSpec((1, tokens, tile), lambda i, j: (i, 0, j)),
                pl.BlockSpec((1, tokens, feats), lambda i, j: (i, 0, 0)),
                pl.BlockSpec((1, tile, feats), lambda i, j: (i, j, 0)),
                pl.BlockSpec((1, tile, rank), lambda i, j: (i, j, 0)),
                pl.BlockSpec((1, rank, feats), lambda i, j: (i, 0, 0)),
                pl.BlockSpec((1, rows, rank), lambda i, j: (i, 0, 0)),
            ],
            out_specs=(
                pl.BlockSpec((1, tile, feats), lambda i, j: (i, j, 0)),
                pl.BlockSpec((1, rows, feats), lambda i, j: (i, 0, 0)),
            ),
            compiler_params=pltpu.CompilerParams(
                dimension_semantics=("arbitrary", "arbitrary"), vmem_limit_bytes=48 * 1024 * 1024
            ),
        )(yfull, context, error_in, ortho, right, own_basis)
        return summed, new_error

    return jax.shard_map(
        body,
        mesh=mesh,
        in_specs=(
            P(None, "dp", "tensor"),
            P(None, ("dp", "tensor"), None),
            P(None, "dp", "tensor"),
            P(None, None, "tensor"),
        ),
        out_specs=(P(None, "dp", "tensor"), P(None, "dp", "tensor")),
        check_vma=False,
    )
```

time: 419 us -> 137 us (0.33)
  waiting for transfers between devices: 279 us -> 0 us
  Pallas kernels: 0 us -> 126 us
  matrix products: 85 us -> 0 us
  other arithmetic: 22 us -> 0 us
  between operations: 13.9 us -> 0.66 us
  blocking collectives: 10.9 us -> 0 us
    psum x2 -> x0, waiting for transfers between devices: 146 us -> none  [the longest x1 75 us: compress(): left_part = lax.psum(left_part, 'dp')]
    pallas_call x0 -> x2, Pallas kernels: none -> 126 us  [the longest x1 103 us: body(): pl.pallas_call(functools.partial(comm_kernel, n_d, n_t), name='low_rank_c...]
    all_gather x2 -> x0, waiting for transfers between devices: 105 us -> none  [the longest x1 86.6 us: compress(): lax.all_gather(out_grad, 'tensor', axis=1, tiled=True)]
    dot_general x6 -> x0, matrix products: 83.7 us -> none  [the longest x1 22.5 us: compress(): jnp.einsum('lre,lde->lrd', right_init, moment, precision=lax.Precision.HI...]
    reduce_scatter x1 -> x0, waiting for transfers between devices: 28.1 us -> none  [compress(): lax.psum_scatter(left_factor, 'tensor', scatter_dimension=2, tiled=True)]
    another operation x7 -> x0, other arithmetic: 21.8 us -> none  [the longest x4 11.9 us: solve_rows(): factor_low = jnp.linalg.cholesky(gram_matrix)]
    psum x1 -> x0, blocking collectives: 10.9 us -> none  [compress(): gram_matrix = lax.psum(gram_of(left_part), 'tensor')]
    unnamed x11 -> x4, local copies, waits for them, and re-layouts: 4.83 us -> 0.01 us
  transfers between devices with their start and end apart: 5 -> 0, of which waited for: 5 -> 0; matrix products, arithmetic and copies ran while one was open for 0% -> 0% of each run, Pallas kernels for 0% -> 0%
where the time goes in v1:
time: 137 us; the launch traced here: 134 us
  Pallas kernels  126 us (92%)
  local copies, waits for them, and re-layouts  7.46 us (5%)
    pallas_call x1, Pallas kernels, body(): pl.pallas_call(functools.partial(comm_kernel, n_d, n_t), name='low_rank_c...  103 us
    pallas_call x1, Pallas kernels, body(): pl.pallas_call(functools.partial(error_kernel, n_d), name='new_error', gr...  22.9 us
    reshape x1, local copies, waits for them, and re-layouts, body(): ortho = jnp.transpose(ortho.reshape(width, layers, rank), (1, 0, 2))  3.41 us
    pallas_call x1, local copies, waits for them, and re-layouts, body(): pl.pallas_call(functools.partial(comm_kernel, n_d, n_t), name='low_rank_c...  3.02 us

profile of v1, /device:TPU:0, one launch (start us, length us, event | category | flops | bytes accessed | tf_op | source)
XLA Modules:
  0.0 134.3 jit_solution(3727616388802766541)
XLA Ops:
  0.6 103.3 %low_rank_chain.1 = (bf16[2,1024,3072]{2,1,0:T(8,128)(2,1)}, f32[3072,128]{1,0:T(8,128)}, bf16[8,16,768]{2,1,0:T(8,128)(2,1)}) custom-call(bf16[2,1024,768]{2,1,0:T(8,128)(2,1)} %x_ref.1, bf16[2,256,3072]{2,1,0:T(8,128)(2,1)} %y_hbm.1, bf16[2,3072,768]{2,1,0:T(8,128)(2,1)} %e_ref.1, f32[2,64,768]{2,1,0:T(8,128)} %r_hbm.1), custom_call_target="tpu_custom_call" | custom-call | tf_op jit(solution)/shard_map/low_rank_chain/pallas_call | solution.py:433
  104.0 3.0 %copy.6 = f32[3072,128]{0,1:T(8,128)} copy(f32[3072,128]{1,0:T(8,128)} %get-tuple-element.8) | data formatting | bytes 3145728 | tf_op jit(solution)/shard_map/low_rank_chain/pallas_call | solution.py:433
  107.0 0.0 copy-start
  107.0 0.0 copy-start.1
  107.0 3.4 %copy.7 = f32[3072,2,64]{2,0,1:T(8,128)} copy(f32[3072,2,64]{0,2,1:T(8,128)} %bitcast.7) | data formatting | bytes 3145728 | tf_op jit(solution)/shard_map/reshape | solution.py:479
  110.4 1.0 dynamic-slice_bitcast_fusion.own_ref
  111.4 0.0 copy-done
  111.4 0.0 copy-done.1
  111.4 22.9 %new_error.1 = (bf16[2,3072,768]{2,1,0:T(8,128)(2,1)}, bf16[2,384,768]{2,1,0:T(8,128)(2,1)}) custom-call(bf16[2,1024,3072]{2,1,0:T(8,128)(2,1)} %get-tuple-element.7.y_ref, bf16[2,1024,768]{2,1,0:T(8,128)(2,1)S(1)} %copy-done, bf16[2,3072,768]{2,1,0:T(8,128)(2,1)} %e_ref.1, f32[2,3072,64]{2,1,0:T(8,128)} %bitcast.6, bf16[2,64,768]{2,1,0:T(8,128)(2,1)S(1)} %bitcast.5, ...), custom_call_target="tpu_custom_call" | custom-call | tf_op jit(solution)/shard_map/new_error/pallas_call | solution.py:484
Async XLA Ops:
  107.0 4.4 %copy-start = (bf16[2,1024,768]{2,1,0:T(8,128)(2,1)S(1)}, bf16[2,1024,768]{2,1,0:T(8,128)(2,1)}, u32[]{:S(2)}) copy-start(bf16[2,1024,768]{2,1,0:T(8,128)(2,1)} %x_ref.1) | copy-start | bytes 9437188
  107.0 4.4 %copy-start.1 = (bf16[8,16,768]{2,1,0:T(8,128)(2,1)S(1)}, bf16[8,16,768]{2,1,0:T(8,128)(2,1)}, u32[]{:S(2)}) copy-start(bf16[8,16,768]{2,1,0:T(8,128)(2,1)} %get-tuple-element.9) | copy-start | bytes 589828

commit v2 on v1

--- a/solution.py
+++ b/solution.py
@@ -11,8 +11,9 @@
 HIGHEST = lax.Precision.HIGHEST
 F32 = jnp.float32
 BF16 = jnp.bfloat16
-LEFT_WIRE = jnp.float32
+WIRE = jnp.bfloat16
 CHUNKS = 8
+PLAN = (2, 3, 1, 6, 0, 16)
 
 
 def split(value):
@@ -55,6 +56,7 @@
     r_hbm,
     yfull,
     ot_ref,
+    own_ref,
     right_ref,
     x_ref,
     y_ref,
@@ -177,7 +179,7 @@
                 forward_copy(i, m).start()
         passed[0] = max(passed[0], min(upto, len(chunks)))
 
-    send_chunks(2)
+    send_chunks(PLAN[0])
     own_copy = remote(y_hbm, yfull.at[:, my_rows, :], f_send.at[0, 0], f_recv.at[0, 0], {"tensor": partner})
     own_copy.start()
     partner_rows = pl.ds(pl.multiple_of(partner * own, own), own)
@@ -193,7 +195,7 @@
             block = x_ref[layer, tile * own : (tile + 1) * own, :]
             high, low = r_parts[layer]
             outs.append(dot(block, high, ((1,), (1,))) + dot(block, low, ((1,), (1,))))
-        pt[tile] = jnp.concatenate(outs, axis=1)
+        pt[tile] = jnp.concatenate(outs, axis=1).astype(pt.dtype)
 
     p_out = []
     for k in range(1, n_t):
@@ -201,7 +203,7 @@
         copy = remote(pt.at[there], pt_in.at[k - 1], p_send.at[k - 1], p_recv.at[k - 1], {"tensor": there})
         copy.start()
         p_out.append(copy)
-    send_chunks(3)
+    send_chunks(PLAN[1])
 
     loads[3].wait()
     loads[2].wait()
@@ -222,9 +224,9 @@
     lax.fori_loop(0, 6, left_of_error, 0)
     for copy in p_out:
         copy.wait()
-    total = pt[t]
+    total = pt[t].astype(F32)
     for k in range(n_t - 1):
-        total = total + pt_in[k]
+        total = total + pt_in[k].astype(F32)
     p_parts = [split(total[:, layer * rank : (layer + 1) * rank]) for layer in range(layers)]
 
     def left_of_tokens(i, carry):
@@ -258,25 +260,26 @@
         copy = remote(lt_send.at[there], lt_in.at[k - 1], d_send.at[k - 1], d_recv.at[k - 1], {"dp": there})
         copy.start()
         d_out.append(copy)
-    send_chunks(4)
-    pass_chunks(2)
+    send_chunks(PLAN[2])
+    pass_chunks(PLAN[0])
     for copy in d_out:
         copy.wait()
     total = lt_send[d].astype(F32)
     for k in range(n_d - 1):
         total = total + lt_in[k].astype(F32)
-    lt_sum[...] = total
+    lt_sum[...] = total.astype(lt_sum.dtype)
+    total = lt_sum[...].astype(F32)
     s_out = []
     for m in range(1, n_y):
         there = lax.rem(t + 2 * m, n_t)
         copy = remote(lt_sum, lt_y.at[m - 1], s_send.at[m - 1], s_recv.at[m - 1], {"tensor": there})
         copy.start()
         s_out.append(copy)
-    send_chunks(3)
     for copy in s_out:
         copy.wait()
+    send_chunks(PLAN[3])
     for m in range(n_y - 1):
-        total = total + lt_y[m]
+        total = total + lt_y[m].astype(F32)
 
     def slot(side, index):
         return ltf.at[pl.ds(pl.multiple_of(side * half + index * piece, piece), piece), :]
@@ -296,8 +299,8 @@
         copy = remote(slot(core, source), slot(core, source), h_send.at[k], h_recv.at[k], {"tensor": partner})
         copy.start()
         h_out.append(copy)
-    send_chunks(3)
-    pass_chunks(7)
+    send_chunks(PLAN[4])
+    pass_chunks(sum(PLAN[:3]))
     for k in range(n_d):
         source = lax.rem(d + n_d - k, n_d)
         remote(
@@ -334,7 +337,7 @@
         for layer in range(layers):
             both = jnp.concatenate(split(basis[:, layer * rank : (layer + 1) * rank]), axis=1)
             q[layer] = q[layer] + dot(y_ref[layer, :, at], both, ((1,), (0,)))
-    q_all[t] = jnp.concatenate([part[:, :rank] + part[:, rank:] for part in q], axis=1)
+    q_all[t] = jnp.concatenate([part[:, :rank] + part[:, rank:] for part in q], axis=1).astype(q_all.dtype)
     q_out = []
     for k in range(1, n_t):
         copy = remote(
@@ -342,7 +345,7 @@
         )
         copy.start()
         q_out.append(copy)
-    send_chunks(len(chunks))
+    send_chunks(PLAN[5])
     for i in range(6):
         at = slice(i * block_rows, (i + 1) * block_rows)
         for layer in range(layers):
@@ -353,12 +356,13 @@
         remote(
             q_all.at[source], q_all.at[source], q_send.at[k - 1], q_recv.at[k - 1], {"tensor": source}
         ).wait_recv()
+    right = [part[:rank] + part[rank:] for part in right]
     for tile in range(tiles):
         value = q_all[tile]
         for layer in range(layers):
-            both = jnp.concatenate(split(value[:, layer * rank : (layer + 1) * rank]), axis=1)
-            right[layer] = right[layer] + dot(both, x_ref[layer, tile * own : (tile + 1) * own, :], ((0,), (0,)))
-    right_rows = jnp.concatenate([part[:rank] + part[rank:] for part in right], axis=0)
+            part = value[:, layer * rank : (layer + 1) * rank]
+            right[layer] = right[layer] + dot(part, x_ref[layer, tile * own : (tile + 1) * own, :], ((0,), (0,)))
+    right_rows = jnp.concatenate(right, axis=0)
     share = layers * rank // n_d
     for j in range(n_d):
         r_send[j] = right_rows[j * share : (j + 1) * share, :].astype(BF16)
@@ -385,6 +389,8 @@
         source = lax.rem(d + n_d - k, n_d)
         remote(r_all.at[source], r_all.at[source], b_send.at[k - 1], b_recv.at[k - 1], {"dp": source}).wait_recv()
     right_ref[...] = r_all[...]
+    own_rows = width // n_d
+    own_ref[...] = ot_ref[pl.ds(pl.multiple_of(d * own_rows, own_rows), own_rows), :]
     own_in.wait_recv()
     own_copy.wait_send()
     own_y.wait()
@@ -399,18 +405,20 @@
 
 def error_kernel(n_d, y_ref, x_ref, e_ref, o_ref, r_ref, own_ref, err_ref, sum_ref):
     layer = pl.program_id(0)
-    rank = r_ref.shape[1]
+    wide = r_ref.shape[0]
+    rank = wide // pl.num_programs(0)
+    of_layer = lax.broadcasted_iota(jnp.int32, (1, wide), 1) // rank == layer
 
     def low_rank(basis):
-        high, low = split(basis)
-        return dot(high, r_ref[0], ((1,), (0,))) + dot(low, r_ref[0], ((1,), (0,)))
+        both = jnp.concatenate(split(jnp.where(of_layer, basis, 0.0)), axis=1)
+        return dot(both, jnp.concatenate([r_ref[...], r_ref[...]], axis=0), ((1,), (0,)))
 
     moment = dot(y_ref[0], x_ref[0], ((0,), (0,))) + e_ref[0].astype(F32)
-    err_ref[0] = (moment - low_rank(o_ref[0]) * (1.0 / n_d)).astype(err_ref.dtype)
+    err_ref[0] = (moment - low_rank(o_ref[...]) * (1.0 / n_d)).astype(err_ref.dtype)
 
     @pl.when(pl.program_id(1) == 0)
     def _():
-        sum_ref[0] = low_rank(own_ref[0]).astype(sum_ref.dtype)
+        sum_ref[0] = low_rank(own_ref[...]).astype(sum_ref.dtype)
 
 
 def solution(mesh):
@@ -426,35 +434,37 @@
         share = wide // n_d
         n_y = n_t // 2
         n_c = layers * CHUNKS
+        rows = width // n_d
         dma = pltpu.SemaphoreType.DMA
         any_spec = pl.BlockSpec(memory_space=pl.ANY)
         vmem_spec = pl.BlockSpec(memory_space=pltpu.VMEM)
         pairs = lambda *shape: [dma(shape), dma(shape)]
-        yfull, ortho, right = pl.pallas_call(
+        yfull, ortho, own_basis, right = pl.pallas_call(
             functools.partial(comm_kernel, n_d, n_t),
             name="low_rank_chain",
             out_shape=(
                 jax.ShapeDtypeStruct((layers, tokens, width), BF16),
                 jax.ShapeDtypeStruct((width, wide), F32),
+                jax.ShapeDtypeStruct((rows, wide), F32),
                 jax.ShapeDtypeStruct((n_d, share, feats), BF16),
             ),
             in_specs=[any_spec] * 4,
-            out_specs=(any_spec, vmem_spec, vmem_spec),
+            out_specs=(any_spec, vmem_spec, vmem_spec, vmem_spec),
             scratch_shapes=[
                 pltpu.VMEM((layers, tokens, feats), BF16),
                 pltpu.VMEM((layers, own, width), BF16),
                 pltpu.VMEM((layers, width, feats), BF16),
                 pltpu.VMEM((layers, rank, feats), F32),
-                pltpu.VMEM((n_t, own, wide), F32),
-                pltpu.VMEM((n_t - 1, own, wide), F32),
-                pltpu.VMEM((n_t, own, wide), F32),
+                pltpu.VMEM((n_t, own, wide), WIRE),
+                pltpu.VMEM((n_t - 1, own, wide), WIRE),
+                pltpu.VMEM((n_t, own, wide), WIRE),
                 pltpu.VMEM((width, wide), F32),
                 pltpu.VMEM((half, wide), F32),
-                pltpu.VMEM((n_d, piece, wide), LEFT_WIRE),
-                pltpu.VMEM((n_d - 1, piece, wide), LEFT_WIRE),
-                pltpu.VMEM((max(n_y - 1, 1), piece, wide), F32),
-                pltpu.VMEM((piece, wide), F32),
-                pltpu.VMEM((width, wide), LEFT_WIRE),
+                pltpu.VMEM((n_d, piece, wide), WIRE),
+                pltpu.VMEM((n_d - 1, piece, wide), WIRE),
+                pltpu.VMEM((max(n_y - 1, 1), piece, wide), WIRE),
+                pltpu.VMEM((piece, wide), WIRE),
+                pltpu.VMEM((width, wide), WIRE),
                 pltpu.VMEM((n_d, share, feats), BF16),
                 pltpu.VMEM((n_d - 1, share, feats), BF16),
                 pltpu.VMEM((n_d, share, feats), BF16),
@@ -476,11 +486,8 @@
                 collective_id=0, has_side_effects=True, vmem_limit_bytes=60 * 1024 * 1024
             ),
         )(context, out_grad, error_in, right_init)
-        ortho = jnp.transpose(ortho.reshape(width, layers, rank), (1, 0, 2))
-        right = right.reshape(layers, rank, feats)
-        rows = width // n_d
-        own_basis = lax.dynamic_slice_in_dim(ortho, lax.axis_index("dp") * rows, rows, 1)
-        tile = width // 6
+        right = right.reshape(wide, feats)
+        tile = width // 3
         new_error, summed = pl.pallas_call(
             functools.partial(error_kernel, n_d),
             name="new_error",
@@ -493,16 +500,16 @@
                 pl.BlockSpec((1, tokens, tile), lambda i, j: (i, 0, j)),
                 pl.BlockSpec((1, tokens, feats), lambda i, j: (i, 0, 0)),
                 pl.BlockSpec((1, tile, feats), lambda i, j: (i, j, 0)),
-                pl.BlockSpec((1, tile, rank), lambda i, j: (i, j, 0)),
-                pl.BlockSpec((1, rank, feats), lambda i, j: (i, 0, 0)),
-                pl.BlockSpec((1, rows, rank), lambda i, j: (i, 0, 0)),
+                pl.BlockSpec((tile, wide), lambda i, j: (j, 0)),
+                pl.BlockSpec((wide, feats), lambda i, j: (0, 0)),
+                pl.BlockSpec((rows, wide), lambda i, j: (0, 0)),
             ],
             out_specs=(
                 pl.BlockSpec((1, tile, feats), lambda i, j: (i, j, 0)),
                 pl.BlockSpec((1, rows, feats), lambda i, j: (i, 0, 0)),
             ),
             compiler_params=pltpu.CompilerParams(
-                dimension_semantics=("arbitrary", "arbitrary"), vmem_limit_bytes=48 * 1024 * 1024
+                dimension_semantics=("arbitrary", "arbitrary"), vmem_limit_bytes=60 * 1024 * 1024
             ),
         )(yfull, context, error_in, ortho, right, own_basis)
         return summed, new_error

time: 137 us -> 109 us (0.80); the launches traced: 134 us -> 108 us
  Pallas kernels: 126 us -> 108 us
  local copies, waits for them, and re-layouts: 7.46 us -> 0 us
    pallas_call x1, Pallas kernels: 103 us -> 87.6 us  [body(): pl.pallas_call(functools.partial(comm_kernel, n_d, n_t), name='low_rank_c...]
    reshape x1 -> x0, local copies, waits for them, and re-layouts: 3.41 us -> none  [body(): ortho = jnp.transpose(ortho.reshape(width, layers, rank), (1, 0, 2))]
    pallas_call x1 -> x0, local copies, waits for them, and re-layouts: 3.02 us -> none  [body(): pl.pallas_call(functools.partial(comm_kernel, n_d, n_t), name='low_rank_c...]
    pallas_call x1, Pallas kernels: 22.9 us -> 20.2 us  [body(): pl.pallas_call(functools.partial(error_kernel, n_d), name='new_error', gr...]
where the time goes in v2:
time: 109 us; the launch traced here: 108 us
  Pallas kernels  108 us (99%)
    pallas_call x1, Pallas kernels, body(): pl.pallas_call(functools.partial(comm_kernel, n_d, n_t), name='low_rank_c...  87.6 us
    pallas_call x1, Pallas kernels, body(): pl.pallas_call(functools.partial(error_kernel, n_d), name='new_error', gr...  20.2 us

profile of v2, /device:TPU:0, one launch (start us, length us, event | category | flops | bytes accessed | tf_op | source)
XLA Modules:
  0.0 108.4 jit_solution(9653532766121029947)
XLA Ops:
  0.6 87.6 %low_rank_chain.1 = (bf16[2,1024,3072]{2,1,0:T(8,128)(2,1)}, f32[3072,128]{1,0:T(8,128)}, f32[384,128]{1,0:T(8,128)}, bf16[8,16,768]{2,1,0:T(8,128)(2,1)}) custom-call(bf16[2,1024,768]{2,1,0:T(8,128)(2,1)} %x_ref.1, bf16[2,256,3072]{2,1,0:T(8,128)(2,1)} %y_hbm.1, bf16[2,3072,768]{2,1,0:T(8,128)(2,1)} %e_ref.1, f32[2,64,768]{2,1,0:T(8,128)} %r_hbm.1), custom_call_target="tpu_custom_call" | custom-call | tf_op jit(solution)/shard_map/low_rank_chain/pallas_call | solution.py:442
  88.2 20.2 %new_error.1 = (bf16[2,3072,768]{2,1,0:T(8,128)(2,1)}, bf16[2,384,768]{2,1,0:T(8,128)(2,1)}) custom-call(bf16[2,1024,3072]{2,1,0:T(8,128)(2,1)} %get-tuple-element.8.y_ref, bf16[2,1024,768]{2,1,0:T(8,128)(2,1)} %x_ref.1, bf16[2,3072,768]{2,1,0:T(8,128)(2,1)} %e_ref.1, f32[3072,128]{1,0:T(8,128)} %get-tuple-element.9.o_ref, bf16[128,768]{1,0:T(8,128)(2,1)} %bitcast.1, ...), custom_call_target="tpu_custom_call" | custom-call | tf_op jit(solution)/shard_map/new_error/pallas_call | solution.py:491
